TPU v7x, 512 devices: a whole 4x4x16 slice. The times are simulated.
512 devices in a mesh: row: 16 (over x, z_lo), col: 32 (over y, z_hi, core).
Axes of the slice: x: 4, y: 4, z: 16 (z_hi: 4, z_lo: 4; z = z_hi * 4 + z_lo), core: 2. Of those that a mesh axis runs over, the one named last changes fastest.
Arguments:
- features: bfloat16 [65536, 256], P(('col', 'row')), may hold values from -6 to 6
- weight: bfloat16 [256, 256], replicated, may hold values from -0.375 to 0.375
- cotangent: bfloat16 [65536, 256], P(('row', 'col')), may hold values from -6 to 6
- block_index: int32 [16, 32, 32], P('row', 'col'), may hold values from 0 to 511, as said below
- block_count: int32 [16, 32], P('row', 'col'), may hold values from 1 to 32, as said below
- block_values: bfloat16 [16, 32, 32, 128, 128], P('row', 'col'), may hold values from -0.125 to 0.125
Outputs:
- hidden_out: bfloat16 [65536, 256], P(('row', 'col'))
- input_grad: bfloat16 [65536, 256], P(('col', 'row'))
- weight_grad: float32 [256, 256], replicated
Inputs may be any that keep to these rules, and one draw needn't show every extreme that they name: `block_index`: the 32 entries of one tile are distinct; slots at or after the tile's count hold blocks that are not used. `block_count`: at least one tile holds exactly 32 blocks.
All inputs are finite; a program needn't handle non-finite values.
Results may differ from a plain program's by a relative error of at most 0.015.
Values may be sent and summed in bfloat16 or wider, within the bound.
A program may use at most 64 MiB of HBM per device.

v0:
```python
import math
import jax
import jax.numpy as jnp
from jax import lax
from jax.sharding import PartitionSpec as P

GROUP = 32


def forward_tile(blocks_in, values, index, count, rows_out):
    ncols = blocks_in.shape[0]
    size = blocks_in.shape[1]
    width = blocks_in.shape[2]
    lanes = jnp.arange(GROUP, dtype=jnp.int32)
    targets = jnp.arange(rows_out, dtype=jnp.int32)

    def forward_advance(group_id, totals):
        start = (group_id * GROUP).astype(jnp.int32)
        live = start + lanes < count
        picked = jnp.take(blocks_in, index % ncols, axis=0)
        product = jnp.einsum("gij,gjd->gid", values, picked, preferred_element_type=jnp.float32)
        selector = ((index // ncols)[None, :] == targets[:, None]) & live[None, :]
        return totals + jnp.einsum(
            "rg,gid->rid", selector.astype(jnp.float32), product, precision=lax.Precision.HIGHEST
        )

    zeros = jnp.zeros((rows_out, size, width), jnp.float32)
    groups = (count + GROUP - 1) // GROUP
    return lax.fori_loop(jnp.int32(0), groups, forward_advance, zeros)


def backward_tile(blocks_grad, values, index, count, cols_out):
    size = blocks_grad.shape[1]
    width = blocks_grad.shape[2]
    lanes = jnp.arange(GROUP, dtype=jnp.int32)
    targets = jnp.arange(cols_out, dtype=jnp.int32)

    def backward_advance(group_id, totals):
        start = (group_id * GROUP).astype(jnp.int32)
        live = start + lanes < count
        picked = jnp.take(blocks_grad, index // cols_out, axis=0)
        product = jnp.einsum("gij,gid->gjd", values, picked, preferred_element_type=jnp.float32)
        selector = ((index % cols_out)[None, :] == targets[:, None]) & live[None, :]
        return totals + jnp.einsum(
            "cg,gjd->cjd", selector.astype(jnp.float32), product, precision=lax.Precision.HIGHEST
        )

    zeros = jnp.zeros((cols_out, size, width), jnp.float32)
    groups = (count + GROUP - 1) // GROUP
    return lax.fori_loop(jnp.int32(0), groups, backward_advance, zeros)


def body(features, weight, cotangent, block_index, block_count, block_values):
    row_total = lax.axis_size("row")
    col_total = lax.axis_size("col")
    rows = features.shape[0]
    width = features.shape[1]
    size = block_values.shape[-1]
    block_rows = rows * col_total // size
    block_cols = rows * row_total // size
    index = block_index[0, 0]
    count = block_count[0, 0]
    values = block_values[0, 0]
    own_projected = jnp.dot(features, weight, preferred_element_type=jnp.float32).astype(
        jnp.bfloat16
    )
    projected = lax.all_gather(own_projected, "row", axis=0, tiled=True)
    partial_out = forward_tile(
        projected.reshape(block_cols, size, width), values, index, count, block_rows
    )
    summed_out = lax.psum_scatter(
        partial_out.reshape(block_rows * size, width).astype(jnp.bfloat16),
        "col",
        scatter_dimension=0,
        tiled=True,
    )
    grad_rows = lax.all_gather(cotangent, "col", axis=0, tiled=True)
    partial_back = backward_tile(
        grad_rows.reshape(block_rows, size, width), values, index, count, block_cols
    )
    partial_back = partial_back.reshape(block_cols * size, width)
    grad_sum = lax.psum_scatter(
        partial_back.astype(jnp.bfloat16), "row", scatter_dimension=0, tiled=True
    ).astype(jnp.float32)
    input_grad = jnp.dot(
        grad_sum, weight.astype(jnp.float32).T, precision=lax.Precision.HIGHEST
    ).astype(jnp.bfloat16)
    term = jnp.dot(features.astype(jnp.float32).T, grad_sum, precision=lax.Precision.HIGHEST)
    total = lax.psum(term, ("row", "col"))
    nodes = rows * row_total * col_total
    weight_grad = total / math.sqrt(nodes)
    return (summed_out, input_grad, weight_grad)


def solution(mesh):
    in_specs = (
        P(("col", "row"), None),
        P(),
        P(("row", "col"), None),
        P("row", "col", None),
        P("row", "col"),
        P("row", "col", None, None, None),
    )
    out_specs = (P(("row", "col"), None), P(("col", "row"), None), P())
    return jax.shard_map(body, mesh=mesh, in_specs=in_specs, out_specs=out_specs, check_vma=False)
```

profile of v0, /device:TPU:6, one launch (start us, length us, event | category | flops | bytes accessed | tf_op | source)
XLA Modules:
  0.0 881.2 jit_solution(7760522335443745997)
XLA Ops:
  7.2 0.0 copy-start
  7.2 0.0 all-gather.5.cloned.1.call-start
  7.2 0.7 all-gather.5.cloned.1.call-update
  7.9 0.0 reduce-scatter.5.cloned.1.call-start
  8.6 0.7 fusion.42
  9.3 0.7 bitcast_sign_fusion.1
  10.0 84.2 %all-gather.5.cloned.1.call-done = bf16[4096,256]{1,0:T(8,128)(2,1)} async-done(((bf16[128,256]{1,0:T(8,128)(2,1)}), bf16[4096,256]{1,0:T(8,128)(2,1)}) %all-gather.5.cloned.1.call-update) | async-done | bytes 2097168 | tf_op jit(solution)/shard_map/all_gather | solution.py:77
  94.2 3.7 gather_fusion.1
  97.8 0.0 copy-start.4
  97.8 0.2 broadcast_in_dim.63
  98.1 0.4 copy-done.4
  98.5 15.7 %while.34 = (s32[]{:T(128)}, f32[16,128,256]{2,0,1:T(8,128)S(1)}, s32[]{:T(128)}, s32[32]{0:T(128)S(1)}, s32[32]{0:T(128)S(1)}, /*index=5*/s32[]{:T(128)}, s32[3...) while((s32[]{:T(128)}, f32[16,128,256]{2,0,1:T(8,128)S(1)}, ...), condition=%wide.region_4.5_spmd.clone, body=%wide.region_3.4_spmd.clone.sunk | while | flops 471336928 | bytes 24118400 | solution.py:50
  98.5 0.7 compare_and_fusion.4
  99.2 4.6 fusion.69
  103.8 5.5 copy.20
  109.3 4.8 fusion.70
  114.2 0.0 copy-start.2
  114.2 2.1 copy.17
  116.3 0.0 reduce-scatter.5.cloned.1.call-update
  116.3 0.0 all-gather.3.cloned.1.call-start
  116.4 0.0 copy-done
  116.4 0.0 copy-done.2
  116.4 0.8 convolution_convert_fusion.1
  117.2 0.0 all-gather.3.cloned.1.call-update
  117.2 0.0 all-reduce.2.cloned.1.call-start
  117.3 78.8 %reduce-scatter.5.cloned.1.call-done = bf16[128,256]{1,0:T(8,128)(2,1)} async-done(((bf16[2048,256]{1,0:T(8,128)(2,1)}), bf16[128,256]{1,0:T(8,128)(2,1)}) %reduce-scatter.5.cloned.1.call-update) | async-done | bytes 65552 | tf_op jit(solution)/shard_map/reduce_scatter | solution.py:82
  196.1 1.8 convolution_bitcast_fusion
  197.8 0.0 all-reduce.2.cloned.1.call-update
  197.9 0.0 reduce-scatter.3.cloned.1.call-start
  197.9 85.1 %all-gather.3.cloned.1.call-done = bf16[2048,256]{1,0:T(8,128)(2,1)} async-done(((bf16[128,256]{1,0:T(8,128)(2,1)}), bf16[2048,256]{1,0:T(8,128)(2,1)}) %all-gather.3.cloned.1.call-update) | async-done | bytes 1048592 | tf_op jit(solution)/shard_map/all_gather | solution.py:67
  283.0 0.0 copy-start.1
  283.0 2.5 broadcast_in_dim.62
  285.5 0.0 copy-done.1
  285.5 18.6 %while.35 = (s32[]{:T(128)}, f32[32,128,256]{2,0,1:T(8,128)}, s32[]{:T(128)}, s32[1,32]{1,0:T(1,128)S(1)}, s32[32]{0:T(128)S(1)}, /*index=5*/s32[1,32]{1,0:T(1,1...) while((s32[]{:T(128)}, f32[32,128,256]{2,0,1:T(8,128)}, ...), condition=%wide.region_1.2_spmd.clone.clone, body=%wide.region_0.1_spmd.clone.clone.sunk | while | flops 673190272 | bytes 32511760 | solution.py:29
  285.5 0.7 compare_and_fusion.5
  286.2 0.7 gather_fusion
  286.9 4.0 fusion.76
  290.9 5.5 copy.21
  296.4 7.7 fusion.78
  304.1 2.5 convert_element_type.25
  306.6 2.5 copy.11
  309.1 0.0 copy-start.3
  309.2 0.0 reduce-scatter.3.cloned.1.call-update
  309.2 0.8 copy-done.3
  310.0 0.8 convolution_convert_fusion
  310.8 441.0 %all-reduce.2.cloned.1.call-done = f32[256,256]{0,1:T(8,128)} async-done(((f32[256,256]{0,1:T(8,128)}), f32[256,256]{0,1:T(8,128)}) %all-reduce.2.cloned.1.call-update) | async-done | bytes 262160 | tf_op jit(solution)/shard_map/psum | solution.py:89
  751.8 1.0 broadcast_multiply_fusion
  752.8 0.8 copy.13
  753.6 121.0 %reduce-scatter.3.cloned.1.call-done = bf16[128,256]{1,0:T(8,128)(2,1)} async-done(((bf16[4096,256]{1,0:T(8,128)(2,1)}), bf16[128,256]{1,0:T(8,128)(2,1)}) %reduce-scatter.3.cloned.1.call-update) | async-done | bytes 65552 | tf_op jit(solution)/shard_map/reduce_scatter | solution.py:71
  (6 shorter events, 0.0 us)
Async XLA Ops:
  7.2 109.2 %copy-start = (bf16[256,256]{1,0:T(8,128)(2,1)S(1)}, bf16[256,256]{1,0:T(8,128)(2,1)}, u32[]{:S(2)}) copy-start(bf16[256,256]{1,0:T(8,128)(2,1)} %param.11) | copy-start | bytes 393220
  7.2 87.0 %all-gather.5.cloned.1.call-start = ((), (), s32[]{:S(2)}) async-start(), calls=%async_computation.4 | async-start | bytes 2162688 | tf_op jit(solution)/shard_map/all_gather | solution.py:77
  7.9 188.2 %reduce-scatter.5.cloned.1.call-start = ((), (), s32[]{:S(2)}) async-start(), calls=%async_computation.5 | async-start | bytes 1114112 | tf_op jit(solution)/shard_map/reduce_scatter | solution.py:82
  97.8 0.7 copy-start.4
  114.2 2.2 copy-start.2
  116.3 166.7 %all-gather.3.cloned.1.call-start = ((), (), s32[]{:S(2)}) async-start(), calls=%async_computation.2 | async-start | bytes 1114112 | tf_op jit(solution)/shard_map/all_gather | solution.py:67
  117.2 634.6 %all-reduce.2.cloned.1.call-start = ((), (), s32[]{:S(2)}) async-start(), calls=%async_computation.6 | async-start | bytes 524288 | tf_op jit(solution)/shard_map/psum | solution.py:89
  197.9 676.8 %reduce-scatter.3.cloned.1.call-start = ((), (), s32[]{:S(2)}) async-start(), calls=%async_computation.3 | async-start | bytes 2162688 | tf_op jit(solution)/shard_map/reduce_scatter | solution.py:71
  283.0 2.5 copy-start.1
  309.1 0.8 copy-start.3
Sparse Core Ops, SparseCore 0:
  11.1 82.9 all-gather.4
  116.4 79.6 reduce-scatter.4
  199.0 83.9 all-gather.2
  289.8 461.9 all-reduce.1
  756.6 117.9 reduce-scatter.2
where the time goes:
time: 882 us; the launch traced here: 881 us
  waiting for transfers between devices  811 us (92%)
  local copies, waits for them, and re-layouts  24.8 us (3%)
  matrix products  24.6 us (3%)
  between operations  14.5 us (2%)
    psum x1, waiting for transfers between devices, body(): total = lax.psum(term, ('row', 'col'))  441 us
    reduce_scatter x1, waiting for transfers between devices, body(): lax.psum_scatter(partial_out.reshape(block_rows * size, width).astype(jnp...  121 us
    all_gather x1, waiting for transfers between devices, body(): projected = lax.all_gather(own_projected, 'row', axis=0, tiled=True)  85.1 us
    all_gather x1, waiting for transfers between devices, body(): grad_rows = lax.all_gather(cotangent, 'col', axis=0, tiled=True)  84.2 us
    reduce_scatter x1, waiting for transfers between devices, body(): lax.psum_scatter(partial_back.astype(jnp.bfloat16), 'row', scatter_dimens...  78.8 us
  transfers between devices with their start and end apart: 5, of which 5 were waited for; matrix products, arithmetic and copies ran while one was open for 4% of the time, Pallas kernels for 0%

commit v1 on v0

--- a/solution.py
+++ b/solution.py
@@ -74,7 +74,9 @@
         scatter_dimension=0,
         tiled=True,
     )
-    grad_rows = lax.all_gather(cotangent, "col", axis=0, tiled=True)
+    grad_rows = jnp.concatenate(
+        lax.all_to_all(jnp.stack([cotangent] * lax.axis_size("col")), "col", 0, 0), axis=0
+    )
     partial_back = backward_tile(
         grad_rows.reshape(block_rows, size, width), values, index, count, block_cols
     )

time: 882 us -> 912 us (1.034)
  starting transfers between devices: 0.2 us -> 18.4 us
  waiting for transfers between devices: 811 us -> 823 us
    all_to_all x0 -> x1, waiting for transfers between devices: none -> 94.1 us  [body(): lax.all_to_all(jnp.stack([cotangent] * lax.axis_size('col')), 'col', 0, 0)]
    all_gather x1 -> x0, waiting for transfers between devices: 84.2 us -> none  [body(): grad_rows = lax.all_gather(cotangent, 'col', axis=0, tiled=True)]
    all_to_all x0 -> x1, starting transfers between devices: none -> 18.2 us  [body(): lax.all_to_all(jnp.stack([cotangent] * lax.axis_size('col')), 'col', 0, 0)]
  transfers between devices with their start and end apart: 5 -> 5, of which waited for: 5 -> 5; matrix products, arithmetic and copies ran while one was open for 4% -> 3% of each run, Pallas kernels for 0% -> 0%
where the time goes in v1:
time: 912 us; the launch traced here: 911 us
  waiting for transfers between devices  823 us (90%)
  local copies, waits for them, and re-layouts  25.2 us (3%)
  matrix products  24.6 us (3%)
  starting transfers between devices  18.4 us (2%)
  between operations  14.5 us (2%)
    psum x1, waiting for transfers between devices, body(): total = lax.psum(term, ('row', 'col'))  441 us
    reduce_scatter x1, waiting for transfers between devices, body(): lax.psum_scatter(partial_out.reshape(block_rows * size, width).astype(jnp...  121 us
    all_to_all x1, waiting for transfers between devices, body(): lax.all_to_all(jnp.stack([cotangent] * lax.axis_size('col')), 'col', 0, 0)  94.1 us
    all_gather x1, waiting for transfers between devices, body(): projected = lax.all_gather(own_projected, 'row', axis=0, tiled=True)  85.1 us
    reduce_scatter x1, waiting for transfers between devices, body(): lax.psum_scatter(partial_back.astype(jnp.bfloat16), 'row', scatter_dimens...  81.9 us
    all_to_all x1, starting transfers between devices, body(): lax.all_to_all(jnp.stack([cotangent] * lax.axis_size('col')), 'col', 0, 0)  18.2 us
  transfers between devices with their start and end apart: 5, of which 5 were waited for; matrix products, arithmetic and copies ran while one was open for 3% of the time, Pallas kernels for 0%

profile of v1, /device:TPU:6, one launch (start us, length us, event | category | flops | bytes accessed | tf_op | source)
XLA Modules:
  0.0 911.0 jit_solution(13227467694994287031)
XLA Ops:
  7.2 0.0 copy-start
  7.2 2.5 stack.2
  9.6 0.0 copy-start.4
  9.6 18.2 %all-to-all-start = ((bf16[32,128,256]{2,1,0:T(8,128)(2,1)}), bf16[32,128,256]{2,1,0:T(8,128)(2,1)S(1)}, u32[]{:S(2)}, u32[]{:S(2)}) async-start(bf16[32,128,256]{2,1,0:T(8,128)(2,1)} %stack.2), calls=%async_computation.1 | async-start | bytes 4194304 | tf_op jit(solution)/shard_map/all_to_all | solution.py:78
  27.9 0.0 reduce-scatter.5.cloned.1.call-start
  28.6 0.0 copy-done.4
  28.7 94.1 %all-to-all-done = bf16[32,128,256]{2,1,0:T(8,128)(2,1)S(1)} async-done(((bf16[32,128,256]{2,1,0:T(8,128)(2,1)}), bf16[32,128,256]{2,1,0:T(8,128)(2,1)S(1)}, u32[]{:S(2)}, u32[]{:S(2)}) %all-to-all-start) | async-done | bytes 2097184 | tf_op jit(solution)/shard_map/all_to_all | solution.py:78
  122.8 2.1 gather_fusion.1
  124.8 0.2 broadcast_in_dim.63
  125.1 15.7 %while.34 = (s32[]{:T(128)}, f32[16,128,256]{2,0,1:T(8,128)S(1)}, s32[]{:T(128)}, s32[32]{0:T(128)S(1)}, s32[32]{0:T(128)S(1)}, /*index=5*/s32[]{:T(128)}, s32[3...) while((s32[]{:T(128)}, f32[16,128,256]{2,0,1:T(8,128)S(1)}, ...), condition=%wide.region_4.5_spmd.clone, body=%wide.region_3.4_spmd.clone.sunk | while | flops 471336928 | bytes 24118400 | solution.py:50
  125.1 0.7 compare_and_fusion.4
  125.8 4.6 fusion.69
  130.4 5.5 copy.20
  135.9 4.8 fusion.70
  140.8 0.0 copy-start.2
  140.8 2.1 copy.17
  142.9 0.0 reduce-scatter.5.cloned.1.call-update
  142.9 0.0 all-gather.2.cloned.1.call-start
  143.0 0.0 copy-done
  143.0 0.0 copy-done.2
  143.0 0.8 convolution_convert_fusion.1
  143.8 0.0 all-gather.2.cloned.1.call-update
  143.8 0.0 all-reduce.2.cloned.1.call-start
  143.9 81.9 %reduce-scatter.5.cloned.1.call-done = bf16[128,256]{1,0:T(8,128)(2,1)} async-done(((bf16[2048,256]{1,0:T(8,128)(2,1)}), bf16[128,256]{1,0:T(8,128)(2,1)}) %reduce-scatter.5.cloned.1.call-update) | async-done | bytes 65552 | tf_op jit(solution)/shard_map/reduce_scatter | solution.py:84
  225.7 1.8 convolution_bitcast_fusion
  227.5 0.0 all-reduce.2.cloned.1.call-update
  227.5 0.0 reduce-scatter.3.cloned.1.call-start
  227.6 85.1 %all-gather.2.cloned.1.call-done = bf16[2048,256]{1,0:T(8,128)(2,1)} async-done(((bf16[128,256]{1,0:T(8,128)(2,1)}), bf16[2048,256]{1,0:T(8,128)(2,1)}) %all-gather.2.cloned.1.call-update) | async-done | bytes 1048592 | tf_op jit(solution)/shard_map/all_gather | solution.py:67
  312.7 0.0 copy-start.1
  312.7 2.5 broadcast_in_dim.62
  315.2 0.0 copy-done.1
  315.2 18.6 %while.35 = (s32[]{:T(128)}, f32[32,128,256]{2,0,1:T(8,128)}, s32[]{:T(128)}, s32[1,32]{1,0:T(1,128)S(1)}, s32[32]{0:T(128)S(1)}, /*index=5*/s32[1,32]{1,0:T(1,1...) while((s32[]{:T(128)}, f32[32,128,256]{2,0,1:T(8,128)}, ...), condition=%wide.region_1.2_spmd.clone.clone, body=%wide.region_0.1_spmd.clone.clone.sunk | while | flops 673190272 | bytes 32511760 | solution.py:29
  315.2 0.7 compare_and_fusion.5
  315.9 0.7 gather_fusion
  316.6 4.0 fusion.76
  320.6 5.5 copy.21
  326.1 7.7 fusion.78
  333.7 2.5 convert_element_type.25
  336.3 2.5 copy.11
  338.8 0.0 copy-start.3
  338.8 0.0 reduce-scatter.3.cloned.1.call-update
  338.8 0.8 copy-done.3
  339.6 0.8 convolution_convert_fusion
  340.4 441.2 %all-reduce.2.cloned.1.call-done = f32[256,256]{0,1:T(8,128)} async-done(((f32[256,256]{0,1:T(8,128)}), f32[256,256]{0,1:T(8,128)}) %all-reduce.2.cloned.1.call-update) | async-done | bytes 262160 | tf_op jit(solution)/shard_map/psum | solution.py:91
  781.6 1.0 broadcast_multiply_fusion
  782.6 0.8 copy.13
  783.4 121.1 %reduce-scatter.3.cloned.1.call-done = bf16[128,256]{1,0:T(8,128)(2,1)} async-done(((bf16[4096,256]{1,0:T(8,128)(2,1)}), bf16[128,256]{1,0:T(8,128)(2,1)}) %reduce-scatter.3.cloned.1.call-update) | async-done | bytes 65552 | tf_op jit(solution)/shard_map/reduce_scatter | solution.py:71
  (8 shorter events, 0.1 us)
Async XLA Ops:
  7.2 135.8 %copy-start = (bf16[256,256]{1,0:T(8,128)(2,1)S(1)}, bf16[256,256]{1,0:T(8,128)(2,1)}, u32[]{:S(2)}) copy-start(bf16[256,256]{1,0:T(8,128)(2,1)} %param.11) | copy-start | bytes 393220
  9.6 19.0 %copy-start.4 = (s32[1,1,32]{2,1,0:T(1,128)S(1)}, s32[1,1,32]{2,1,0:T(1,128)}, u32[]{:S(2)}) copy-start(s32[1,1,32]{2,1,0:T(1,128)} %param.13) | copy-start | bytes 388
  9.6 113.1 %all-to-all-start = ((bf16[32,128,256]{2,1,0:T(8,128)(2,1)}), bf16[32,128,256]{2,1,0:T(8,128)(2,1)S(1)}, u32[]{:S(2)}, u32[]{:S(2)}) async-start(bf16[32,128,256]{2,1,0:T(8,128)(2,1)} %stack.2), calls=%async_computation.1 | async-start | bytes 4194304 | tf_op jit(solution)/shard_map/all_to_all | solution.py:78
  27.9 197.8 %reduce-scatter.5.cloned.1.call-start = ((), (), s32[]{:S(2)}) async-start(), calls=%async_computation.5 | async-start | bytes 1114112 | tf_op jit(solution)/shard_map/reduce_scatter | solution.py:84
  140.8 2.2 copy-start.2
  142.9 169.7 %all-gather.2.cloned.1.call-start = ((), (), s32[]{:S(2)}) async-start(), calls=%async_computation.3 | async-start | bytes 1114112 | tf_op jit(solution)/shard_map/all_gather | solution.py:67
  143.8 637.8 %all-reduce.2.cloned.1.call-start = ((), (), s32[]{:S(2)}) async-start(), calls=%async_computation.6 | async-start | bytes 524288 | tf_op jit(solution)/shard_map/psum | solution.py:91
  227.5 677.0 %reduce-scatter.3.cloned.1.call-start = ((), (), s32[]{:S(2)}) async-start(), calls=%async_computation.4 | async-start | bytes 2162688 | tf_op jit(solution)/shard_map/reduce_scatter | solution.py:71
  312.7 2.5 copy-start.1
  338.8 0.8 copy-start.3
Sparse Core Ops, SparseCore 0:
  143.0 82.6 reduce-scatter.4
  228.6 84.0 all-gather.1
  319.6 461.9 all-reduce.1
  786.4 118.0 reduce-scatter.2
